TPU v7x, 32 devices: a whole 2x2x4 slice. The times are simulated.
32 devices in a mesh: dp: 8 (over y, x, core), mp: 4 (over z).
Axes of the slice: x: 2, y: 2, z: 4, core: 2. Of those that a mesh axis runs over, the one named last changes fastest.
Arguments:
- tokens: bfloat16 [16384, 768], P('dp'), may hold values from -6 to 6
- cotangent: bfloat16 [16384, 768], P('dp'), may hold values from -6 to 6
- random_blocks: int32 [16, 12, 14, 3], P('dp', 'mp'), may hold values from 1 to 14
- query_weight: bfloat16 [768, 768], P(None, 'mp'), may hold values from -0.21875 to 0.21875
- query_bias: bfloat16 [768], P('mp'), may hold values from -3 to 3
- key_weight: bfloat16 [768, 768], P(None, 'mp'), may hold values from -0.21875 to 0.21875
- value_weight: bfloat16 [768, 768], P(None, 'mp'), may hold values from -0.21875 to 0.21875
- value_bias: bfloat16 [768], P('mp'), may hold values from -0.59765625 to 0.59765625
- out_weight: bfloat16 [768, 768], P('mp'), may hold values from -1.75 to 1.75
- out_bias: bfloat16 [768], replicated, may hold values from -2 to 2
- attn_gain: bfloat16 [768], replicated, may hold values from 0.099609375 to 1.8984375
- attn_shift: bfloat16 [768], replicated, may hold values from -2 to 2
- up_weight: bfloat16 [768, 3072], P(None, 'mp'), may hold values from -0.21875 to 0.21875
- up_bias: bfloat16 [3072], P('mp'), may hold values from -3 to 3
- down_weight: bfloat16 [3072, 768], P('mp'), may hold values from -0.21875 to 0.21875
- down_bias: bfloat16 [768], replicated, may hold values from -2 to 2
- mlp_gain: bfloat16 [768], replicated, may hold values from 0.099609375 to 1.8984375
- mlp_shift: bfloat16 [768], replicated, may hold values from -2 to 2
Outputs:
- layer_out: float32 [16384, 768], P('dp')
- tokens_grad: float32 [16384, 768], P('dp')
- grad_query_weight: float32 [768, 768], P(None, 'mp')
- grad_query_bias: float32 [768], P('mp')
- grad_key_weight: float32 [768, 768], P(None, 'mp')
- grad_value_weight: float32 [768, 768], P(None, 'mp')
- grad_value_bias: float32 [768], P('mp')
- grad_out_weight: float32 [768, 768], P('mp')
- grad_out_bias: float32 [768], replicated
- grad_attn_gain: float32 [768], replicated
- grad_attn_shift: float32 [768], replicated
- grad_up_weight: float32 [768, 3072], P(None, 'mp')
- grad_up_bias: float32 [3072], P('mp')
- grad_down_weight: float32 [3072, 768], P('mp')
- grad_down_bias: float32 [768], replicated
- grad_mlp_gain: float32 [768], replicated
- grad_mlp_shift: float32 [768], replicated
All inputs are finite; a program needn't handle non-finite values.
Results may differ from a plain program's by a relative error of at most 0.014.
The roundings to bfloat16 on the way count: a program that leaves them out, or rounds other values in their place, can miss the bound.
Values sent between devices are 32-bit elements; how exact they have to be, the bound alone decides.
A program may use at most 256 MiB of HBM per device.

v0:
```python
import jax
import jax.numpy as jnp
from jax import lax
from jax.sharding import PartitionSpec as P

HEAD_DIM = 64
BLOCK = 64
LEN = 1024
EPSILON = 1e-05
SCALING = 0.125
MIDDLE_FORMS = ("shmqd,shmkd->shmqk", "shmqk,shmkd->shmqd", "shmqk,shmqd->shmkd")
GLOBAL_FORMS = ("shgqd,shkd->shgqk", "shgqk,shkd->shgqd", "shgqk,shgqd->shkd")


def contract_rows(left, right):
    return lax.dot_general(
        left, right, (((0,), (0,)), ((), ())), preferred_element_type=jnp.float32
    )


def apply_rows(left, weight):
    return lax.dot_general(
        left, weight, (((1,), (1,)), ((), ())), preferred_element_type=jnp.float32
    )


def norm_stats(summed):
    row_mean = jnp.mean(summed, -1, keepdims=True)
    centered = summed - row_mean
    scaling = lax.rsqrt(jnp.mean(centered * centered, -1, keepdims=True) + EPSILON)
    return (centered * scaling, scaling)


def norm_back(grad_result, normed, scaling, scale_gain):
    grad_normed = grad_result * scale_gain
    inner_mean = jnp.mean(grad_normed, -1, keepdims=True)
    cross_mean = jnp.mean(grad_normed * normed, -1, keepdims=True)
    return scaling * (grad_normed - inner_mean - normed * cross_mean)


def finish_norm(partial_sum, residual, bias_value, which):
    if which == "attn":
        summed = lax.psum(partial_sum, "mp")
    else:
        summed = lax.psum(partial_sum, "mp")
    result = norm_stats(residual + (summed + bias_value))
    return result


def to_heads(flat, seq_count):
    head_count = flat.shape[1] // HEAD_DIM
    return flat.reshape(seq_count, LEN // BLOCK, BLOCK, head_count, HEAD_DIM).transpose(
        0, 3, 1, 2, 4
    )


def from_heads(split):
    seq_count, head_count, block_count, block_rows, head_dim = split.shape
    return split.transpose(0, 2, 3, 1, 4).reshape(
        seq_count * block_count * block_rows, head_count * head_dim
    )


def key_blocks(random_blocks):
    block_count = LEN // BLOCK
    middle = jnp.arange(1, block_count - 1, dtype=jnp.int32)
    fixed = jnp.stack(
        [
            middle - 1,
            middle,
            middle + 1,
            jnp.zeros_like(middle),
            jnp.full_like(middle, block_count - 1),
        ],
        1,
    )
    fixed = jnp.broadcast_to(fixed, random_blocks.shape[:2] + fixed.shape)
    return jnp.concatenate([fixed, random_blocks], 3)


def pick_blocks(blocks, chosen):
    picked = jax.vmap(jax.vmap(lambda source, listed: source[listed]))(blocks, chosen)
    seq_count, head_count, middle_count, listed_count, block_rows, head_dim = picked.shape
    return picked.reshape(seq_count, head_count, middle_count, listed_count * block_rows, head_dim)


def soft_forward(queries, key_rows, value_rows, forms):
    scores = jnp.einsum(forms[0], queries, key_rows, preferred_element_type=jnp.float32) * SCALING
    highest = jnp.max(scores, -1, keepdims=True)
    summed = jnp.sum(jnp.exp(scores - highest), -1, keepdims=True)
    logsum = highest + jnp.log(summed)
    soft_low = jnp.exp(scores - logsum).astype(jnp.bfloat16)
    return (jnp.einsum(forms[1], soft_low, value_rows, preferred_element_type=jnp.float32), logsum)


def soft_back(queries, key_rows, value_rows, logsum, grad_out, forms):
    scores = jnp.einsum(forms[0], queries, key_rows, preferred_element_type=jnp.float32) * SCALING
    soft = jnp.exp(scores - logsum)
    grad_soft = jnp.einsum(forms[0], grad_out, value_rows, preferred_element_type=jnp.float32)
    row_inner = jnp.sum(soft * grad_soft, -1, keepdims=True)
    grad_scores = (soft * (grad_soft - row_inner)).astype(jnp.bfloat16)
    grad_values = jnp.einsum(
        forms[2], soft.astype(jnp.bfloat16), grad_out, preferred_element_type=jnp.float32
    )
    grad_queries = (
        jnp.einsum(forms[1], grad_scores, key_rows, preferred_element_type=jnp.float32) * SCALING
    )
    grad_keys = (
        jnp.einsum(forms[2], grad_scores, queries, preferred_element_type=jnp.float32) * SCALING
    )
    return (grad_queries, grad_keys, grad_values)


def global_rows(split):
    block_count = split.shape[2]
    return jnp.stack([split[:, :, 0], split[:, :, block_count - 1]], 2)


def flat_keys(split):
    seq_count, head_count, block_count, block_rows, head_dim = split.shape
    return split.reshape(seq_count, head_count, block_count * block_rows, head_dim)


def attend_all(queries, key_rows, value_rows, chosen):
    block_count = queries.shape[2]
    out_middle, log_middle = soft_forward(
        queries[:, :, 1 : block_count - 1],
        pick_blocks(key_rows, chosen),
        pick_blocks(value_rows, chosen),
        MIDDLE_FORMS,
    )
    out_global, log_global = soft_forward(
        global_rows(queries), flat_keys(key_rows), flat_keys(value_rows), GLOBAL_FORMS
    )
    attended = jnp.concatenate([out_global[:, :, 0:1], out_middle, out_global[:, :, 1:2]], 2)
    return (attended, (log_middle, log_global))


def attend_back(queries, key_rows, value_rows, chosen, logsums, grad_out):
    block_count = queries.shape[2]
    grad_middle_q, grad_listed_k, grad_listed_v = soft_back(
        queries[:, :, 1 : block_count - 1],
        pick_blocks(key_rows, chosen),
        pick_blocks(value_rows, chosen),
        logsums[0],
        grad_out[:, :, 1 : block_count - 1],
        MIDDLE_FORMS,
    )
    grad_global_q, grad_all_k, grad_all_v = soft_back(
        global_rows(queries),
        flat_keys(key_rows),
        flat_keys(value_rows),
        logsums[1],
        global_rows(grad_out),
        GLOBAL_FORMS,
    )
    onehot = (chosen[..., None] == jnp.arange(block_count, dtype=jnp.int32)).astype(jnp.float32)
    split_shape = chosen.shape + (queries.shape[3], queries.shape[4])
    grad_keys = jnp.einsum(
        "shmcn,shmckd->shnkd",
        onehot,
        grad_listed_k.reshape(split_shape),
        precision=lax.Precision.HIGHEST,
    ) + grad_all_k.reshape(queries.shape)
    grad_values = jnp.einsum(
        "shmcn,shmckd->shnkd",
        onehot,
        grad_listed_v.reshape(split_shape),
        precision=lax.Precision.HIGHEST,
    ) + grad_all_v.reshape(queries.shape)
    grad_queries = jnp.concatenate(
        [grad_global_q[:, :, 0:1], grad_middle_q, grad_global_q[:, :, 1:2]], 2
    )
    return (grad_queries, grad_keys, grad_values)


def column_sum(values_low):
    return jnp.sum(values_low.astype(jnp.float32), 0)


def on_device(
    tokens,
    cotangent,
    random_blocks,
    query_weight,
    query_bias,
    key_weight,
    value_weight,
    value_bias,
    out_weight,
    out_bias,
    attn_gain,
    attn_shift,
    up_weight,
    up_bias,
    down_weight,
    down_bias,
    mlp_gain,
    mlp_shift,
):
    seq_count = tokens.shape[0] // LEN
    residual = tokens.astype(jnp.float32)
    queries = (
        jnp.dot(tokens, query_weight, preferred_element_type=jnp.float32)
        + query_bias.astype(jnp.float32)
    ).astype(jnp.bfloat16)
    key_rows = jnp.dot(tokens, key_weight, preferred_element_type=jnp.float32).astype(jnp.bfloat16)
    value_rows = (
        jnp.dot(tokens, value_weight, preferred_element_type=jnp.float32)
        + value_bias.astype(jnp.float32)
    ).astype(jnp.bfloat16)
    query_heads = to_heads(queries, seq_count)
    key_heads = to_heads(key_rows, seq_count)
    value_heads = to_heads(value_rows, seq_count)
    chosen = key_blocks(random_blocks)
    attended, logsums = attend_all(query_heads, key_heads, value_heads, chosen)
    attended_low = from_heads(attended).astype(jnp.bfloat16)
    attn_partial = jnp.dot(attended_low, out_weight, preferred_element_type=jnp.float32)
    normed_attn, scale_attn = finish_norm(
        attn_partial, residual, out_bias.astype(jnp.float32), "attn"
    )
    gain_one = attn_gain.astype(jnp.float32)
    hidden = normed_attn * gain_one + attn_shift.astype(jnp.float32)
    hidden_low = hidden.astype(jnp.bfloat16)
    up_value = jnp.dot(hidden_low, up_weight, preferred_element_type=jnp.float32) + up_bias.astype(
        jnp.float32
    )
    active, gelu_pull = jax.vjp(lambda entry: jax.nn.gelu(entry, approximate=True), up_value)
    active_low = active.astype(jnp.bfloat16)
    mlp_partial = jnp.dot(active_low, down_weight, preferred_element_type=jnp.float32)
    normed_mlp, scale_mlp = finish_norm(mlp_partial, hidden, down_bias.astype(jnp.float32), "mlp")
    gain_two = mlp_gain.astype(jnp.float32)
    layer_out = normed_mlp * gain_two + mlp_shift.astype(jnp.float32)
    grad_result = cotangent.astype(jnp.float32)
    grad_mlp_gain = jnp.sum(grad_result * normed_mlp, 0)
    grad_mlp_shift = jnp.sum(grad_result, 0)
    grad_mlp_in = norm_back(grad_result, normed_mlp, scale_mlp, gain_two)
    grad_mlp_low = grad_mlp_in.astype(jnp.bfloat16)
    grad_down_bias = column_sum(grad_mlp_low)
    grad_down_weight = contract_rows(active_low, grad_mlp_low)
    grad_active = apply_rows(grad_mlp_low, down_weight)
    grad_up_value = gelu_pull(grad_active)[0].astype(jnp.bfloat16)
    grad_up_bias = column_sum(grad_up_value)
    grad_up_weight = contract_rows(hidden_low, grad_up_value)
    mlp_terms = (
        grad_up_weight,
        grad_up_bias,
        grad_down_weight,
        grad_down_bias,
        grad_mlp_gain,
        grad_mlp_shift,
    )
    back_hidden = lax.psum(apply_rows(grad_up_value, up_weight), "mp")
    grad_hidden = grad_mlp_in + back_hidden
    grad_attn_gain = jnp.sum(grad_hidden * normed_attn, 0)
    grad_attn_shift = jnp.sum(grad_hidden, 0)
    grad_attn_in = norm_back(grad_hidden, normed_attn, scale_attn, gain_one)
    grad_attn_low = grad_attn_in.astype(jnp.bfloat16)
    grad_out_bias = column_sum(grad_attn_low)
    grad_out_weight = contract_rows(attended_low, grad_attn_low)
    grad_attended = apply_rows(grad_attn_low, out_weight).astype(jnp.bfloat16)
    grad_q_heads, grad_k_heads, grad_v_heads = attend_back(
        query_heads, key_heads, value_heads, chosen, logsums, to_heads(grad_attended, seq_count)
    )
    grad_queries = from_heads(grad_q_heads).astype(jnp.bfloat16)
    grad_keys = from_heads(grad_k_heads).astype(jnp.bfloat16)
    grad_values = from_heads(grad_v_heads).astype(jnp.bfloat16)
    grad_query_weight = contract_rows(tokens, grad_queries)
    grad_query_bias = column_sum(grad_queries)
    grad_key_weight = contract_rows(tokens, grad_keys)
    grad_value_weight = contract_rows(tokens, grad_values)
    grad_value_bias = column_sum(grad_values)
    back_tokens = lax.psum(
        apply_rows(grad_queries, query_weight)
        + apply_rows(grad_keys, key_weight)
        + apply_rows(grad_values, value_weight),
        "mp",
    )
    tokens_grad = grad_attn_in + back_tokens
    attn_terms = (
        grad_query_weight,
        grad_query_bias,
        grad_key_weight,
        grad_value_weight,
        grad_value_bias,
        grad_out_weight,
        grad_out_bias,
        grad_attn_gain,
        grad_attn_shift,
    )
    summed_all = lax.psum(attn_terms + mlp_terms, "dp")
    attn_terms = summed_all[:9]
    mlp_terms = summed_all[9:]
    return (
        layer_out,
        tokens_grad,
        attn_terms[0],
        attn_terms[1],
        attn_terms[2],
        attn_terms[3],
        attn_terms[4],
        attn_terms[5],
        attn_terms[6],
        attn_terms[7],
        attn_terms[8],
        mlp_terms[0],
        mlp_terms[1],
        mlp_terms[2],
        mlp_terms[3],
        mlp_terms[4],
        mlp_terms[5],
    )


def solution(mesh):
    return jax.shard_map(
        on_device,
        mesh=mesh,
        in_specs=(
            P("dp", None),
            P("dp", None),
            P("dp", "mp", None, None),
            P(None, "mp"),
            P("mp"),
            P(None, "mp"),
            P(None, "mp"),
            P("mp"),
            P("mp", None),
            P(),
            P(),
            P(),
            P(None, "mp"),
            P("mp"),
            P("mp", None),
            P(),
            P(),
            P(),
        ),
        out_specs=(
            P("dp", None),
            P("dp", None),
            P(None, "mp"),
            P("mp"),
            P(None, "mp"),
            P(None, "mp"),
            P("mp"),
            P("mp", None),
            P(),
            P(),
            P(),
            P(None, "mp"),
            P("mp"),
            P("mp", None),
            P(),
            P(),
            P(),
        ),
        check_vma=False,
    )
```

profile of v0, /device:TPU:0, one launch (start us, length us, event | category | flops | bytes accessed | tf_op | source)
XLA Modules:
  0.0 1423.7 jit_solution(11912262535709834846)
XLA Ops:
  38.2 14.0 gather_fusion
  52.2 15.7 %gather_fusion.1 = bf16[672,64,64]{2,1,0:T(8,128)(2,1)} fusion(bf16[2,3,16,64,64]{4,3,2,1,0:T(8,128)(2,1)} %bitcast.159, s32[672]{0:T(1024)S(1)} %reshape.248), kind=kCustom, calls=%fused_computation.1 | custom fusion | bytes 11018112 | tf_op jit(solution)/shard_map/vmap(vmap())/gather | solution.py:82
  67.9 12.1 multiply_reduce_fusion.1
  80.1 5.9 exponential_reduce_fusion
  86.0 9.5 convolution_convert_fusion.2
  104.8 225.6 %all-reduce.8.cloned.1.call-done = f32[2048,768]{1,0:T(8,128)} async-done(((f32[2048,768]{1,0:T(8,128)}), f32[2048,768]{1,0:T(8,128)}) %all-reduce.8.cloned.1.call-update) | async-done | bytes 6291472 | tf_op jit(solution)/shard_map/psum | solution.py:43
  330.4 4.6 fusion.64
  344.7 5.9 fusion.61
  351.2 221.2 %all-reduce.10.cloned.1.call-done = f32[2048,768]{1,0:T(8,128)} async-done(((f32[2048,768]{1,0:T(8,128)}), f32[2048,768]{1,0:T(8,128)}) %all-reduce.10.cloned.1.call-update) | async-done | bytes 6291472 | tf_op jit(solution)/shard_map/psum | solution.py:45
  572.5 5.7 fusion.63
  583.7 4.9 convert_reduce_fusion.1
  588.7 7.1 convert_reduce_fusion.2
  602.8 221.1 %all-reduce.12.cloned.1.call-done = f32[2048,768]{1,0:T(8,128)} async-done(((f32[2048,768]{1,0:T(8,128)}), f32[2048,768]{1,0:T(8,128)}) %all-reduce.12.cloned.1.call-update) | async-done | bytes 6291472 | tf_op jit(solution)/shard_map/psum | solution.py:253
  823.9 9.1 multiply_reduce_fusion.2
  833.0 5.2 convert_reduce_fusion.3
  846.0 12.5 multiply_reduce_fusion
  858.4 10.9 fusion.22
  877.9 7.1 multiply_convert_fusion
  887.2 7.2 broadcast_multiply_fusion
  921.5 16.6 %reshape.244 = f32[2,3,14,8,64,64]{4,3,5,2,1,0:T(8,128)} reshape(f32[2,3,14,512,64]{3,4,2,1,0:T(8,128)} %broadcast_multiply_fusion) | data formatting | bytes 22020096 | tf_op jit(solution)/shard_map/reshape | solution.py:162
  938.1 26.6 %copy.68 = f32[2,3,14,8,64,64]{5,2,3,4,1,0:T(8,128)} copy(f32[2,3,14,8,64,64]{4,3,5,2,1,0:T(8,128)} %reshape.244) | data formatting | bytes 22020096 | tf_op jit(solution)/shard_map/reshape | solution.py:162
  964.8 15.6 %fusion.21 = bf16[2,16,64,3,64]{4,1,2,3,0:T(8,128)(2,1)} fusion(f32[2,3,16,64,64]{4,2,3,1,0:T(8,128)} %copy.70, f32[2,3,14,8,64,64]{5,2,3,4,1,0:T(8,128)} %copy.68, s32[2,3,14,8]{2,3,1,0:T(8,128)S(1)} %pad_add_fusion), kind=kOutput, calls=%fused_computation.69 | convolution fusion | flops 529279488 | bytes 13372032 | tf_op jit(solution)/shard_map/shmcn,shmckd->shnkd/dot_general | solution.py:159
  991.0 16.6 %reshape.246 = f32[2,3,14,8,64,64]{4,3,5,2,1,0:T(8,128)} reshape(f32[2,3,14,512,64]{3,4,2,1,0:T(8,128)} %fusion.22) | data formatting | bytes 22020096 | tf_op jit(solution)/shard_map/reshape | solution.py:168
  1007.6 26.4 %copy.73 = f32[2,3,14,8,64,64]{5,2,3,4,1,0:T(8,128)} copy(f32[2,3,14,8,64,64]{4,3,5,2,1,0:T(8,128)} %reshape.246) | data formatting | bytes 22020096 | tf_op jit(solution)/shard_map/reshape | solution.py:168
  1034.1 17.9 %convert_reduce_fusion.4 = (f32[3,64]{1,0:T(4,128)S(1)}, bf16[2,3,16,64,64]{4,2,3,1,0:T(8,128)(2,1)}) fusion(f32[2,3,16,64,64]{4,2,3,1,0:T(8,128)} %copy.75, f32[2,3,14,8,64,64]{5,2,3,4,1,0:T(8,128)} %copy.73, s32[2,3,14,8]{2,3,1,0:T(8,128)S(1)} %pad_add_fusion), kind=kOutput, calls=%fused_computation.51 | convolution fusion | flops 530065728 | bytes 13372800 | tf_op jit(solution)/shard_map/shmcn,shmckd->shnkd/dot_general | solution.py:165
  1058.9 8.6 add_add_fusion
  1067.8 6.9 fusion.74
  1074.7 9.7 fusion.50
  1091.7 26.0 %all-reduce = (f32[192]{0:T(256)}, f32[192]{0:T(256)}, f32[768]{0:T(1024)}, f32[768]{0:T(1024)}, f32[768]{0:T(1024)}, /*index=5*/f32[768]{0:T(1024)}, f32[768]{0:T(1024)}, f32[768]{0:T(1024)}, f32[768]{0:T(1024)}) all-reduce(f32[192]{0:T(256)S(1)} %reduce_sum.206, f32[192]{0:T(256)S(1)} %reduce_sum.208, ...), channel_id=1, replica_groups=mesh['dp'=8,'mp'=4] {'dp'}, use_global_device_ids=true, to_apply=%region_20.0 | all-reduce | flops 5760 | bytes 46080 | tf_op jit(solution)/shard_map/psum | solution.py:291
  1117.8 171.7 %all-reduce.14.cloned.1.call-done = f32[2048,768]{1,0:T(8,128)} async-done(((f32[2048,768]{1,0:T(8,128)}), f32[2048,768]{1,0:T(8,128)}) %all-reduce.14.cloned.1.call-update) | async-done | bytes 6291472 | tf_op jit(solution)/shard_map/psum | solution.py:273
  1289.4 8.1 add.232
  1297.5 108.7 %all-reduce.16.cloned.1.call-done = (f32[768,192]{0,1:T(8,128)}, f32[768,192]{0,1:T(8,128)}, f32[768,192]{0,1:T(8,128)}, f32[192,768]{1,0:T(8,128)}, f32[768,768]{1,0:T(8,128)}, /*index=5*/f32[768,768]{1,0:T(8,128)}) async-done(((f32[768,192]{0,1:T(8,128)}, f32[768,192]{0,1:T(8,128)}, f32[768,192]{0,1:T(8,128)}, f32[192,768]{1,0:T(8,128)}, f32[768,768]{1,0:T(8,128)}, /*index=5*/f32[768,768]{1,0:T(8,128)}), ...) | async-done | bytes 7077904 | tf_op jit(solution)/shard_map/psum | solution.py:291
  (239 shorter events, 144.0 us)
Async XLA Ops:
  7.2 337.5 %copy-start = (bf16[768,768]{1,0:T(8,128)(2,1)S(1)}, bf16[768,768]{1,0:T(8,128)(2,1)}, u32[]{:S(2)}) copy-start(bf16[768,768]{1,0:T(8,128)(2,1)} %param.32) | copy-start | bytes 3538948
  7.2 323.2 %all-reduce.8.cloned.1.call-start = ((), (), s32[]{:S(2)}) async-start(), calls=%async_computation | async-start | bytes 12582912 | tf_op jit(solution)/shard_map/psum | solution.py:43
  17.7 17.1 %copy-start.26 = (bf16[2,3,1,64,64]{4,3,2,1,0:T(8,128)(2,1)}, bf16[2,3,1,64,64]{4,3,2,1,0:T(8,128)(2,1)S(1)}, u32[]{:S(2)}) copy-start(bf16[2,3,1,64,64]{4,3,2,1,0:T(8,128)(2,1)S(1)} %get-tuple-element.52) | copy-start | bytes 147460
  17.8 17.1 %copy-start.28 = (bf16[2,3,1,64,64]{4,3,2,1,0:T(8,128)(2,1)}, bf16[2,3,1,64,64]{4,3,2,1,0:T(8,128)(2,1)S(1)}, u32[]{:S(2)}) copy-start(bf16[2,3,1,64,64]{4,3,2,1,0:T(8,128)(2,1)S(1)} %get-tuple-element.53) | copy-start | bytes 147460
  17.8 9.0 copy-start.31
  52.2 15.7 %copy-start.21 = (bf16[2,16,64,3,64]{4,2,1,3,0:T(8,128)(2,1)S(1)}, bf16[2,16,64,3,64]{4,2,1,3,0:T(8,128)(2,1)}, u32[]{:S(2)}) copy-start(bf16[2,16,64,3,64]{4,2,1,3,0:T(8,128)(2,1)} %copy.48) | copy-start | bytes 2359300
  95.5 5.3 copy-start.25
  104.7 467.8 %all-reduce.10.cloned.1.call-start = ((), (), s32[]{:S(2)}) async-start(), calls=%async_computation.1 | async-start | bytes 12582912 | tf_op jit(solution)/shard_map/psum | solution.py:45
  104.8 483.9 %copy-start.44 = (f32[768]{0:T(1024)}, f32[768]{0:T(1024)S(1)}, u32[]{:S(2)}) copy-start(f32[768]{0:T(1024)S(1)} %convert_element_type.146) | copy-start | bytes 9220
  350.5 473.4 %all-reduce.12.cloned.1.call-start = ((), (), s32[]{:S(2)}) async-start(), calls=%async_computation.2 | async-start | bytes 12582912 | tf_op jit(solution)/shard_map/psum | solution.py:253
  580.0 8.6 slice-start.8
  588.6 7.1 copy-start.11
  602.0 687.4 %all-reduce.14.cloned.1.call-start = ((), (), s32[]{:S(2)}) async-start(), calls=%async_computation.3 | async-start | bytes 12582912 | tf_op jit(solution)/shard_map/psum | solution.py:273
  858.4 12.0 copy-start.8
  858.4 12.0 copy-start.35
  874.3 10.8 slice-start.5
  877.9 7.1 slice-start.6
  877.9 7.1 slice-start.7
  901.8 16.0 %copy-start.15 = (bf16[2048,192]{0,1:T(8,128)(2,1)}, bf16[2048,192]{0,1:T(8,128)(2,1)S(1)}, u32[]{:S(2)}) copy-start(bf16[2048,192]{0,1:T(8,128)(2,1)S(1)} %convert_element_type.160) | copy-start | bytes 2359300
  910.0 7.9 copy-start.30
  964.8 22.5 %copy-start.32 = (bf16[768,192]{0,1:T(8,128)(2,1)S(1)}, bf16[768,192]{0,1:T(8,128)(2,1)}, u32[]{:S(2)}) copy-start(bf16[768,192]{0,1:T(8,128)(2,1)} %param.23) | copy-start | bytes 884740
  987.3 20.3 %copy-start.17 = (bf16[2048,192]{0,1:T(8,128)(2,1)}, bf16[2048,192]{0,1:T(8,128)(2,1)S(1)}, u32[]{:S(2)}) copy-start(bf16[2048,192]{0,1:T(8,128)(2,1)S(1)} %convert_element_type.163) | copy-start | bytes 2359300
  1034.1 24.8 %copy-start.33 = (bf16[768,192]{0,1:T(8,128)(2,1)S(1)}, bf16[768,192]{0,1:T(8,128)(2,1)}, u32[]{:S(2)}) copy-start(bf16[768,192]{0,1:T(8,128)(2,1)} %param.24) | copy-start | bytes 884740
  1058.9 8.6 copy-start.19
  1067.5 7.2 copy-start.45
  1067.5 338.7 %all-reduce.16.cloned.1.call-start = ((), (), s32[]{:S(2)}) async-start(), calls=%async_computation.4 | async-start | bytes 14155776 | tf_op jit(solution)/shard_map/psum | solution.py:291
  1074.7 9.7 copy-start.10
  1074.7 9.7 copy-start.16
  1074.7 11.4 copy-start.18
  1406.2 7.9 copy-start.24
  1406.2 9.3 copy-start.23
  1406.2 10.7 copy-start.1
  (39 other events, 107.6 us)
Sparse Core Ops, SparseCore 0:
  104.8 225.5 all-reduce.7
  350.7 221.7 all-reduce.9
  602.1 221.7 all-reduce.11
  1067.7 221.7 all-reduce.13
  1294.5 111.6 all-reduce.15
where the time goes:
time: 1430 us; the launch traced here: 1420 us
  waiting for transfers between devices  948 us (66%)
  local copies, waits for them, and re-layouts  202 us (14%)
  matrix products  169 us (12%)
  other arithmetic  62.7 us (4%)
  blocking collectives  26 us (2%)
  between operations  14.9 us (1%)
    psum x2, waiting for transfers between devices, finish_norm(): summed = lax.psum(partial_sum, 'mp')  447 us
    psum x1, waiting for transfers between devices, on_device(): back_hidden = lax.psum(apply_rows(grad_up_value, up_weight), 'mp')  221 us
    psum x1, waiting for transfers between devices, on_device(): lax.psum(apply_rows(grad_queries, query_weight) + apply_rows(grad_keys, k...  172 us
    psum x1, waiting for transfers between devices, on_device(): summed_all = lax.psum(attn_terms + mlp_terms, 'dp')  109 us
    reshape x2, local copies, waits for them, and re-layouts, attend_back(): grad_listed_k.reshape(split_shape)  43.2 us
    reshape x2, local copies, waits for them, and re-layouts, attend_back(): grad_listed_v.reshape(split_shape)  43 us
    gather x3, local copies, waits for them, and re-layouts, pick_blocks(): source[listed]  29.7 us
    dot_general x6, matrix products, apply_rows(): lax.dot_general(left, weight, (((1,), (1,)), ((), ())), preferred_element...  28.7 us
  transfers between devices with their start and end apart: 5, of which 5 were waited for; matrix products, arithmetic and copies ran while one was open for 2% of the time, Pallas kernels for 0%

commit v1 on v0

--- a/solution.py
+++ b/solution.py
@@ -250,7 +250,9 @@
         grad_mlp_gain,
         grad_mlp_shift,
     )
-    back_hidden = lax.psum(apply_rows(grad_up_value, up_weight), "mp")
+    own = apply_rows(grad_up_value, up_weight)
+    parts = lax.all_gather(own, "mp", axis=0, tiled=False)
+    back_hidden = parts.sum(axis=0)
     grad_hidden = grad_mlp_in + back_hidden
     grad_attn_gain = jnp.sum(grad_hidden * normed_attn, 0)
     grad_attn_shift = jnp.sum(grad_hidden, 0)

time: 1430 us -> 1650 us (1.15)
  waiting for transfers between devices: 948 us -> 1150 us
    all_gather x0 -> x1, waiting for transfers between devices: none -> 423 us  [on_device(): parts = lax.all_gather(own, 'mp', axis=0, tiled=False)]
    psum x1 -> x0, waiting for transfers between devices: 221 us -> none  [on_device(): back_hidden = lax.psum(apply_rows(grad_up_value, up_weight), 'mp')]
where the time goes in v1:
time: 1650 us; the launch traced here: 1640 us
  waiting for transfers between devices  1150 us (70%)
  local copies, waits for them, and re-layouts  202 us (12%)
  matrix products  169 us (10%)
  other arithmetic  75.2 us (5%)
  blocking collectives  26.4 us (2%)
    psum x2, waiting for transfers between devices, finish_norm(): summed = lax.psum(partial_sum, 'mp')  447 us
    all_gather x1, waiting for transfers between devices, on_device(): parts = lax.all_gather(own, 'mp', axis=0, tiled=False)  423 us
    psum x1, waiting for transfers between devices, on_device(): lax.psum(apply_rows(grad_queries, query_weight) + apply_rows(grad_keys, k...  171 us
    psum x1, waiting for transfers between devices, on_device(): summed_all = lax.psum(attn_terms + mlp_terms, 'dp')  109 us
    reshape x2, local copies, waits for them, and re-layouts, attend_back(): grad_listed_v.reshape(split_shape)  43.4 us
    reshape x2, local copies, waits for them, and re-layouts, attend_back(): grad_listed_k.reshape(split_shape)  43 us
  transfers between devices with their start and end apart: 5, of which 5 were waited for; matrix products, arithmetic and copies ran while one was open for 2% of the time, Pallas kernels for 0%

profile of v1, /device:TPU:0, one launch (start us, length us, event | category | flops | bytes accessed | tf_op | source)
XLA Modules:
  0.0 1637.7 jit_solution(13251574246561691506)
XLA Ops:
  38.2 13.9 gather_fusion
  52.1 15.5 gather_fusion.1
  67.6 12.2 multiply_reduce_fusion.1
  79.8 5.9 exponential_reduce_fusion
  85.7 9.5 convolution_convert_fusion.2
  104.5 225.6 %all-reduce.7.cloned.1.call-done = f32[2048,768]{1,0:T(8,128)} async-done(((f32[2048,768]{1,0:T(8,128)}), f32[2048,768]{1,0:T(8,128)}) %all-reduce.7.cloned.1.call-update) | async-done | bytes 6291472 | tf_op jit(solution)/shard_map/psum | solution.py:43
  344.4 5.9 fusion.61
  351.0 221.2 %all-reduce.9.cloned.1.call-done = f32[2048,768]{1,0:T(8,128)} async-done(((f32[2048,768]{1,0:T(8,128)}), f32[2048,768]{1,0:T(8,128)}) %all-reduce.9.cloned.1.call-update) | async-done | bytes 6291472 | tf_op jit(solution)/shard_map/psum | solution.py:45
  572.2 5.7 fusion.63
  583.5 4.9 convert_reduce_fusion.1
  588.4 7.1 convert_reduce_fusion.2
  602.6 423.4 %all-gather.3.cloned.1.call-done = f32[8192,768]{1,0:T(8,128)} async-done(((f32[2048,768]{1,0:T(8,128)}), f32[8192,768]{1,0:T(8,128)}) %all-gather.3.cloned.1.call-update) | async-done | bytes 25165840 | tf_op jit(solution)/shard_map/all_gather | solution.py:254
  1026.0 13.0 reduce_sum.210
  1039.1 8.7 multiply_reduce_fusion.2
  1047.8 5.2 convert_reduce_fusion.3
  1060.7 12.7 multiply_reduce_fusion
  1073.5 10.9 fusion.22
  1093.0 6.9 multiply_convert_fusion
  1102.1 7.2 broadcast_multiply_fusion
  1136.4 16.6 %reshape.244 = f32[2,3,14,8,64,64]{4,3,5,2,1,0:T(8,128)} reshape(f32[2,3,14,512,64]{3,4,2,1,0:T(8,128)} %broadcast_multiply_fusion) | data formatting | bytes 22020096 | tf_op jit(solution)/shard_map/reshape | solution.py:162
  1153.0 26.4 %copy.68 = f32[2,3,14,8,64,64]{5,2,3,4,1,0:T(8,128)} copy(f32[2,3,14,8,64,64]{4,3,5,2,1,0:T(8,128)} %reshape.244) | data formatting | bytes 22020096 | tf_op jit(solution)/shard_map/reshape | solution.py:162
  1179.5 15.6 fusion.21
  1205.7 17.0 %reshape.246 = f32[2,3,14,8,64,64]{4,3,5,2,1,0:T(8,128)} reshape(f32[2,3,14,512,64]{3,4,2,1,0:T(8,128)} %fusion.22) | data formatting | bytes 22020096 | tf_op jit(solution)/shard_map/reshape | solution.py:168
  1222.7 26.4 %copy.73 = f32[2,3,14,8,64,64]{5,2,3,4,1,0:T(8,128)} copy(f32[2,3,14,8,64,64]{4,3,5,2,1,0:T(8,128)} %reshape.246) | data formatting | bytes 22020096 | tf_op jit(solution)/shard_map/reshape | solution.py:168
  1249.2 17.6 %convert_reduce_fusion.4 = (f32[3,64]{1,0:T(4,128)S(1)}, bf16[2,3,16,64,64]{4,2,3,1,0:T(8,128)(2,1)}) fusion(f32[2,3,16,64,64]{4,2,3,1,0:T(8,128)} %copy.75, f32[2,3,14,8,64,64]{5,2,3,4,1,0:T(8,128)} %copy.73, s32[2,3,14,8]{2,3,1,0:T(8,128)S(1)} %pad_add_fusion), kind=kOutput, calls=%fused_computation.51 | convolution fusion | flops 530065728 | bytes 13372800 | tf_op jit(solution)/shard_map/shmcn,shmckd->shnkd/dot_general | solution.py:165
  1273.7 8.6 add_add_fusion
  1282.5 6.9 fusion.74
  1289.4 9.7 fusion.50
  1306.4 26.4 %all-reduce = (f32[192]{0:T(256)}, f32[192]{0:T(256)}, f32[768]{0:T(1024)}, f32[768]{0:T(1024)}, f32[768]{0:T(1024)}, /*index=5*/f32[768]{0:T(1024)}, f32[768]{0:T(1024)}, f32[768]{0:T(1024)}, f32[768]{0:T(1024)}) all-reduce(f32[192]{0:T(256)S(1)} %reduce_sum.216, f32[192]{0:T(256)S(1)} %reduce_sum.218, ...), channel_id=1, replica_groups=mesh['dp'=8,'mp'=4] {'dp'}, use_global_device_ids=true, to_apply=%region_20.0 | all-reduce | flops 5760 | bytes 46080 | tf_op jit(solution)/shard_map/psum | solution.py:293
  1332.8 170.6 %all-reduce.11.cloned.1.call-done = f32[2048,768]{1,0:T(8,128)} async-done(((f32[2048,768]{1,0:T(8,128)}), f32[2048,768]{1,0:T(8,128)}) %all-reduce.11.cloned.1.call-update) | async-done | bytes 6291472 | tf_op jit(solution)/shard_map/psum | solution.py:275
  1503.4 8.1 add.230
  1511.5 108.7 %all-reduce.13.cloned.1.call-done = (f32[768,192]{0,1:T(8,128)}, f32[768,192]{0,1:T(8,128)}, f32[768,192]{0,1:T(8,128)}, f32[192,768]{1,0:T(8,128)}, f32[768,768]{1,0:T(8,128)}, /*index=5*/f32[768,768]{1,0:T(8,128)}) async-done(((f32[768,192]{0,1:T(8,128)}, f32[768,192]{0,1:T(8,128)}, f32[768,192]{0,1:T(8,128)}, f32[192,768]{1,0:T(8,128)}, f32[768,768]{1,0:T(8,128)}, /*index=5*/f32[768,768]{1,0:T(8,128)}), ...) | async-done | bytes 7077904 | tf_op jit(solution)/shard_map/psum | solution.py:293
  (240 shorter events, 148.7 us)
Async XLA Ops:
  7.2 337.3 %copy-start = (bf16[768,768]{1,0:T(8,128)(2,1)S(1)}, bf16[768,768]{1,0:T(8,128)(2,1)}, u32[]{:S(2)}) copy-start(bf16[768,768]{1,0:T(8,128)(2,1)} %param.32) | copy-start | bytes 3538948
  7.2 322.9 %all-reduce.7.cloned.1.call-start = ((), (), s32[]{:S(2)}) async-start(), calls=%async_computation | async-start | bytes 12582912 | tf_op jit(solution)/shard_map/psum | solution.py:43
  17.7 17.1 %copy-start.26 = (bf16[2,3,1,64,64]{4,3,2,1,0:T(8,128)(2,1)}, bf16[2,3,1,64,64]{4,3,2,1,0:T(8,128)(2,1)S(1)}, u32[]{:S(2)}) copy-start(bf16[2,3,1,64,64]{4,3,2,1,0:T(8,128)(2,1)S(1)} %get-tuple-element.52) | copy-start | bytes 147460
  17.7 17.1 %copy-start.28 = (bf16[2,3,1,64,64]{4,3,2,1,0:T(8,128)(2,1)}, bf16[2,3,1,64,64]{4,3,2,1,0:T(8,128)(2,1)S(1)}, u32[]{:S(2)}) copy-start(bf16[2,3,1,64,64]{4,3,2,1,0:T(8,128)(2,1)S(1)} %get-tuple-element.53) | copy-start | bytes 147460
  17.7 9.0 copy-start.31
  52.1 15.5 copy-start.21
  95.2 5.3 copy-start.25
  104.4 467.8 %all-reduce.9.cloned.1.call-start = ((), (), s32[]{:S(2)}) async-start(), calls=%async_computation.1 | async-start | bytes 12582912 | tf_op jit(solution)/shard_map/psum | solution.py:45
  104.5 483.9 %copy-start.44 = (f32[768]{0:T(1024)}, f32[768]{0:T(1024)S(1)}, u32[]{:S(2)}) copy-start(f32[768]{0:T(1024)S(1)} %convert_element_type.146) | copy-start | bytes 9220
  350.3 675.7 %all-gather.3.cloned.1.call-start = ((), (), s32[]{:S(2)}) async-start(), calls=%async_computation.3 | async-start | bytes 31457280 | tf_op jit(solution)/shard_map/all_gather | solution.py:254
  579.8 8.6 slice-start.8
  588.4 7.1 copy-start.11
  601.8 901.6 %all-reduce.11.cloned.1.call-start = ((), (), s32[]{:S(2)}) async-start(), calls=%async_computation.2 | async-start | bytes 12582912 | tf_op jit(solution)/shard_map/psum | solution.py:275
  1073.4 12.0 copy-start.8
  1073.4 12.0 copy-start.35
  1089.3 10.6 slice-start.5
  1093.0 7.0 slice-start.6
  1093.0 7.0 slice-start.7
  1116.7 16.0 copy-start.15
  1124.9 7.9 copy-start.30
  1179.5 22.5 %copy-start.32 = (bf16[768,192]{0,1:T(8,128)(2,1)S(1)}, bf16[768,192]{0,1:T(8,128)(2,1)}, u32[]{:S(2)}) copy-start(bf16[768,192]{0,1:T(8,128)(2,1)} %param.23) | copy-start | bytes 884740
  1202.0 20.7 %copy-start.17 = (bf16[2048,192]{0,1:T(8,128)(2,1)}, bf16[2048,192]{0,1:T(8,128)(2,1)S(1)}, u32[]{:S(2)}) copy-start(bf16[2048,192]{0,1:T(8,128)(2,1)S(1)} %convert_element_type.163) | copy-start | bytes 2359300
  1249.2 24.5 %copy-start.33 = (bf16[768,192]{0,1:T(8,128)(2,1)S(1)}, bf16[768,192]{0,1:T(8,128)(2,1)}, u32[]{:S(2)}) copy-start(bf16[768,192]{0,1:T(8,128)(2,1)} %param.24) | copy-start | bytes 884740
  1273.6 8.6 copy-start.19
  1282.2 7.2 copy-start.45
  1282.3 338.0 %all-reduce.13.cloned.1.call-start = ((), (), s32[]{:S(2)}) async-start(), calls=%async_computation.4 | async-start | bytes 14155776 | tf_op jit(solution)/shard_map/psum | solution.py:293
  1289.4 9.7 copy-start.10
  1289.4 9.7 copy-start.16
  1289.4 11.4 copy-start.18
  1620.2 7.9 copy-start.24
  1620.2 9.3 copy-start.23
  1620.2 10.7 copy-start.1
  (39 other events, 107.7 us)
Sparse Core Ops, SparseCore 0:
  104.5 225.5 all-reduce.6
  350.5 221.7 all-reduce.8
  602.0 424.0 all-gather.2
  1282.4 221.0 all-reduce.10
  1508.5 111.6 all-reduce.12
